TPU v7x, 32 devices: a whole 2x2x4 slice. The times are simulated.
32 devices in a mesh: blk: 4 (over z), virt: 8 (over y, x, core).
Axes of the slice: x: 2, y: 2, z: 4, core: 2. Of those that a mesh axis runs over, the one named last changes fastest.
Arguments:
- integrals: bfloat16 [512, 16, 4096], P(('blk', 'virt')), may hold values from -0.09375 to 0.09375
- amplitudes: bfloat16 [256, 4096], P('blk'), may hold values from -6 to 6
- readers: int32 [512], P(('blk', 'virt')), may hold values from 0 to 7, as said below
- row_slots: int32 [512], P(('blk', 'virt')), may hold values from 0 to 3
- tile_mask: int32 [512, 4], P(('blk', 'virt')), may hold values 0 or 1
- virt_energy: float32 [2048], P(('blk', 'virt')), may hold values from 1 to 3
- occ_energy: float32 [1200], replicated, may hold values from -1 to -0.25
- pair_first: int32 [256], replicated, may hold values from 0 to 1199
- pair_second: int32 [256], replicated, may hold values from 0 to 1199
Outputs:
- update: bfloat16 [2048, 256], P(('blk', 'virt'))
Inputs may be any that keep to these rules, and one draw needn't show every extreme that they name: `readers`: each tile names a reader on the virt axis in the same blk row as its generating device; one device names one reader at most 4 times, and in every blk row some reader is named 4 times by every device of that row.
All inputs are finite; a program needn't handle non-finite values. No bound on the sum of `tile_mask` on one device may be relied on, other than what follows from the above.
Results may differ from a plain program's by a relative error of at most 0.001.
Values may be sent and summed in bfloat16 or wider, within the bound.
A program may use at most 64 MiB of HBM per device.

v0:
```python
import jax
import jax.numpy as jnp
from jax import lax
from jax.sharding import PartitionSpec as P


def body(
    integrals,
    amplitudes,
    readers,
    row_slots,
    tile_mask,
    virt_energy,
    occ_energy,
    pair_first,
    pair_second,
):
    virt_count = lax.axis_size("virt")
    blk_count = lax.axis_size("blk")
    generated = integrals.shape[0]
    tile_rows = integrals.shape[1]
    panel_rows = amplitudes.shape[0]
    capacity = max(1, 2 * generated // virt_count)
    slot_count = virt_count * capacity
    row_blocks = virt_energy.shape[0] // tile_rows
    tile_order = jnp.arange(generated, dtype=jnp.int32)
    same_reader = readers[:, None] == readers[None, :]
    earlier = tile_order[None, :] < tile_order[:, None]
    within = jnp.sum((same_reader & earlier).astype(jnp.int32), axis=1)
    position = readers * capacity + within
    placing = jnp.arange(slot_count, dtype=jnp.int32)[:, None] == position[None, :]
    filled = jnp.any(placing, axis=1)
    source_tile = jnp.sum(placing.astype(jnp.int32) * tile_order[None, :], axis=1)
    row_hot = (row_slots[:, None] == jnp.arange(row_blocks, dtype=jnp.int32)[None, :]).astype(
        jnp.float32
    )
    mask_float = tile_mask.astype(jnp.float32)
    sent_tiles = jnp.where(
        filled[:, None, None], integrals[source_tile], jnp.zeros((), jnp.bfloat16)
    )
    coefficient = (row_hot[:, :, None] * mask_float[:, None, :]).reshape(
        generated, row_blocks * blk_count
    )
    sent_coef = jnp.where(filled[:, None], coefficient[source_tile], 0.0).astype(jnp.bfloat16)
    got_tiles, got_coef = (
        lax.all_to_all(sent_tiles, "virt", split_axis=0, concat_axis=0, tiled=True),
        lax.all_to_all(sent_coef, "virt", split_axis=0, concat_axis=0, tiled=True),
    )
    got_coef = got_coef.astype(jnp.float32).reshape(slot_count, row_blocks, blk_count)
    panel = lax.all_gather(amplitudes, "blk", axis=0, tiled=True)
    column_count = panel.shape[0]
    column_panel = jnp.arange(column_count, dtype=jnp.int32) // panel_rows
    columns = jnp.einsum(
        "srk,kp->srp",
        got_coef,
        (jnp.arange(blk_count, dtype=jnp.int32)[:, None] == column_panel[None, :]).astype(
            jnp.float32
        ),
        precision=lax.Precision.HIGHEST,
    )
    product = jnp.einsum("stw,pw->stp", got_tiles, panel, preferred_element_type=jnp.float32)
    summed_panel = jnp.einsum("srp,stp->rtp", columns, product, precision=lax.Precision.HIGHEST)
    summed = summed_panel.reshape(row_blocks * tile_rows, column_count)
    levels = jnp.arange(occ_energy.shape[0], dtype=jnp.int32)[None, :]
    first_energy = jnp.sum(
        jnp.where(pair_first[:, None] == levels, occ_energy[None, :], 0.0), axis=1
    )
    second_energy = jnp.sum(
        jnp.where(pair_second[:, None] == levels, occ_energy[None, :], 0.0), axis=1
    )
    denominator = virt_energy[:, None] - first_energy[None, :] - second_energy[None, :]
    return (summed / denominator).astype(jnp.bfloat16)


def solution(mesh):
    placed = (
        P(("blk", "virt"), None, None),
        P("blk", None),
        P(("blk", "virt")),
        P(("blk", "virt")),
        P(("blk", "virt"), None),
        P(("blk", "virt")),
        P(),
        P(),
        P(),
    )
    return jax.shard_map(
        body, mesh=mesh, in_specs=placed, out_specs=P(("blk", "virt"), None), check_vma=False
    )
```

profile of v0, /device:TPU:0, one launch (start us, length us, event | category | flops | bytes accessed | tf_op | source)
XLA Modules:
  0.0 97.9 jit_solution(15406979760878977125)
XLA Ops:
  6.5 1.0 %convert_reduce_fusion = s32[16]{0:T(128)S(1)} fusion(s32[16]{0:T(128)} %param.11), kind=kLoop, calls=%fused_computation.16 | loop fusion | flops 1264 | bytes 128 | tf_op jit(solution)/shard_map/reduce_sum | solution.py:29
  7.5 0.7 multiply_add_fusion
  8.2 0.1 select_reduce_fusion.2
  8.3 0.1 fusion.5
  8.4 0.7 convert_element_type.25
  9.1 0.7 fusion.10
  9.8 0.1 copy.20
  9.8 0.1 broadcast_in_dim.44
  9.9 0.6 gather_fusion.1
  10.5 0.7 select_convert_fusion
  11.2 5.2 %all-to-all-start.1 = ((bf16[8,4,16]{2,1,0:T(4,128)(2,1)}), bf16[8,4,16]{2,1,0:T(4,128)(2,1)S(1)}, u32[]{:S(2)}, u32[]{:S(2)}) async-start(bf16[8,4,16]{2,1,0:T(4,128)(2,1)} %select_convert_fusion), calls=%async_computation.1 | async-start | bytes 16384 | tf_op jit(solution)/shard_map/all_to_all | solution.py:47
  16.4 2.8 %gather_fusion = bf16[32,16,4096]{2,1,0:T(8,128)(2,1)} fusion(bf16[16,16,4096]{2,1,0:T(8,128)(2,1)S(1)} %copy-done, s32[1024]{0:T(1024)S(1)} %pad_clamp_fusion), kind=kCustom, calls=%fused_computation | custom fusion | bytes 8388736 | tf_op jit(solution)/shard_map/gather | solution.py:39
  19.2 4.5 %broadcast_select_fusion = bf16[32,16,4096]{2,1,0:T(8,128)(2,1)} fusion(bf16[32,16,4096]{2,1,0:T(8,128)(2,1)} %gather_fusion, pred[32]{0:T(512)(128)(4,1)S(1)} %fusion.5), kind=kLoop, calls=%fused_computation.2 | loop fusion | flops 2097152 | bytes 8388640 | tf_op jit(solution)/shard_map/jit(_where)/select_n | solution.py:38
  23.7 4.7 %all-to-all-start = ((bf16[32,16,4096]{2,1,0:T(8,128)(2,1)}), bf16[32,16,4096]{2,1,0:T(8,128)(2,1)}, u32[]{:S(2)}, u32[]{:S(2)}) async-start(bf16[32,16,4096]{2,1,0:T(8,128)(2,1)} %broadcast_select_fusion), calls=%async_computation | async-start | bytes 8388608 | tf_op jit(solution)/shard_map/all_to_all | solution.py:46
  28.4 0.7 all-gather.2.cloned.1.call-update
  29.2 0.4 select_reduce_fusion.1
  29.6 0.1 fusion.3
  29.8 0.2 copy.23
  30.0 48.4 %all-gather.2.cloned.1.call-done = bf16[256,4096]{1,0:T(8,128)(2,1)} async-done(((bf16[64,4096]{1,0:T(8,128)(2,1)}), bf16[256,4096]{1,0:T(8,128)(2,1)}) %all-gather.2.cloned.1.call-update) | async-done | bytes 2097168 | tf_op jit(solution)/shard_map/all_gather | solution.py:50
  78.4 4.1 %fusion = f32[32,16,256]{2,1,0:T(8,128)S(1)} fusion(bf16[32,16,4096]{2,1,0:T(8,128)(2,1)} %all-to-all-done, bf16[256,4096]{1,0:T(8,128)(2,1)} %all-gather.2.cloned.1.call-done), kind=kOutput, calls=%fused_computation.3 | convolution fusion | flops 1073741824 | bytes 6815744 | tf_op jit(solution)/shard_map/stw,pw->stp/dot_general | solution.py:61
  82.6 2.6 %copy.22 = f32[32,16,256]{0,1,2:T(8,128)} copy(f32[32,16,256]{2,1,0:T(8,128)S(1)} %fusion) | data formatting | bytes 1048576 | tf_op jit(solution)/shard_map/stw,pw->stp/dot_general | solution.py:61
  85.2 5.0 %convolution_bitcast_fusion = f32[4,16,256]{1,0,2:T(4,128)S(1)} fusion(f32[32,16,256]{0,1,2:T(8,128)} %copy.22, f32[32,4,256]{0,1,2:T(4,128)S(1)} %copy.23), kind=kOutput, calls=%fused_computation.5 | convolution fusion | flops 6291456 | bytes 720896 | tf_op jit(solution)/shard_map/srp,stp->rtp/dot_general | solution.py:62
  90.2 0.2 copy.24
  90.4 0.7 fusion.2
  (18 shorter events, 0.2 us)
Async XLA Ops:
  6.5 9.8 %copy-start = (bf16[16,16,4096]{2,1,0:T(8,128)(2,1)S(1)}, bf16[16,16,4096]{2,1,0:T(8,128)(2,1)}, u32[]{:S(2)}) copy-start(bf16[16,16,4096]{2,1,0:T(8,128)(2,1)} %param.9) | copy-start | bytes 6291460
  11.2 12.5 %all-to-all-start.1 = ((bf16[8,4,16]{2,1,0:T(4,128)(2,1)}), bf16[8,4,16]{2,1,0:T(4,128)(2,1)S(1)}, u32[]{:S(2)}, u32[]{:S(2)}) async-start(bf16[8,4,16]{2,1,0:T(4,128)(2,1)} %select_convert_fusion), calls=%async_computation.1 | async-start | bytes 16384 | tf_op jit(solution)/shard_map/all_to_all | solution.py:47
  23.7 5.5 %copy-start.1 = (f32[1200]{0:T(1024)S(1)}, f32[1200]{0:T(1024)}, u32[]{:S(2)}) copy-start(f32[1200]{0:T(1024)} %param.15) | copy-start | bytes 14404
  23.7 5.5 %copy-start.2 = (s32[256]{0:T(256)S(1)}, s32[256]{0:T(256)}, u32[]{:S(2)}) copy-start(s32[256]{0:T(256)} %param.16) | copy-start | bytes 3076
  23.7 5.5 %copy-start.3 = (s32[256]{0:T(256)S(1)}, s32[256]{0:T(256)}, u32[]{:S(2)}) copy-start(s32[256]{0:T(256)} %param.17) | copy-start | bytes 3076
  23.7 54.8 %all-to-all-start = ((bf16[32,16,4096]{2,1,0:T(8,128)(2,1)}), bf16[32,16,4096]{2,1,0:T(8,128)(2,1)}, u32[]{:S(2)}, u32[]{:S(2)}) async-start(bf16[32,16,4096]{2,1,0:T(8,128)(2,1)} %broadcast_select_fusion), calls=%async_computation | async-start | bytes 8388608 | tf_op jit(solution)/shard_map/all_to_all | solution.py:46
  28.4 50.1 %all-gather.2.cloned.1.call-start = ((), (), s32[]{:S(2)}) async-start(), calls=%async_computation.2 | async-start | bytes 2621440 | tf_op jit(solution)/shard_map/all_gather | solution.py:50
  85.2 5.2 %copy-start.4 = (f32[64]{0:T(128)S(1)}, f32[64]{0:T(128)}, u32[]{:S(2)}) copy-start(f32[64]{0:T(128)} %param.14) | copy-start | bytes 772
Sparse Core Ops, SparseCore 0:
  30.8 47.6 all-gather.1
where the time goes:
time: 98.4 us; the launch traced here: 97.9 us
  waiting for transfers between devices  49.1 us (50%)
  between operations  13.5 us (14%)
  starting transfers between devices  9.9 us (10%)
  other arithmetic  9.47 us (10%)
  matrix products  9.28 us (9%)
  local copies, waits for them, and re-layouts  6.7 us (7%)
    all_gather x1, waiting for transfers between devices, body(): panel = lax.all_gather(amplitudes, 'blk', axis=0, tiled=True)  48.4 us
    all_to_all x1, starting transfers between devices, body(): lax.all_to_all(sent_coef, 'virt', split_axis=0, concat_axis=0, tiled=True)  5.17 us
    dot_general x1, matrix products, body(): jnp.einsum('srp,stp->rtp', columns, product, precision=lax.Precision.HIGH...  4.99 us
    all_to_all x1, starting transfers between devices, body(): lax.all_to_all(sent_tiles, 'virt', split_axis=0, concat_axis=0, tiled=True)  4.69 us
    select_n x1, other arithmetic, body(): jnp.where(filled[:, None, None], integrals[source_tile], jnp.zeros((), jn...  4.5 us
    dot_general x1, matrix products, body(): jnp.einsum('stw,pw->stp', got_tiles, panel, preferred_element_type=jnp.fl...  4.15 us
    gather x1, local copies, waits for them, and re-layouts, body(): integrals[source_tile]  2.79 us
    dot_general x1, local copies, waits for them, and re-layouts, body(): jnp.einsum('stw,pw->stp', got_tiles, panel, preferred_element_type=jnp.fl...  2.62 us
  transfers between devices with their start and end apart: 3, of which 1 were waited for; matrix products, arithmetic and copies ran while one was open for 8% of the time, Pallas kernels for 0%

commit v1 on v0

--- a/solution.py
+++ b/solution.py
@@ -2,6 +2,24 @@
 import jax.numpy as jnp
 from jax import lax
 from jax.sharding import PartitionSpec as P
+
+
+def in_order(tiles, dim):
+    shape = list(tiles.shape[1:])
+    shape[dim] *= tiles.shape[0]
+    return jnp.moveaxis(tiles, 0, dim).reshape(shape)
+
+
+def doubled(shard, axis):
+    devices = lax.axis_size(axis)
+    blocks = shard[None]
+    for level in range(devices.bit_length() - 1):
+        bit = 1 << level
+        theirs = lax.ppermute(blocks, axis, [(i, i ^ bit) for i in range(devices)])
+        both = jnp.stack([blocks, theirs])
+        upper = lax.axis_index(axis) >> level & 1
+        blocks = jnp.where(upper == 0, both, both[::-1]).reshape(-1, *shard.shape)
+    return blocks
 
 
 def body(
@@ -47,7 +65,7 @@
         lax.all_to_all(sent_coef, "virt", split_axis=0, concat_axis=0, tiled=True),
     )
     got_coef = got_coef.astype(jnp.float32).reshape(slot_count, row_blocks, blk_count)
-    panel = lax.all_gather(amplitudes, "blk", axis=0, tiled=True)
+    panel = in_order(doubled(amplitudes, "blk"), 0)
     column_count = panel.shape[0]
     column_panel = jnp.arange(column_count, dtype=jnp.int32) // panel_rows
     columns = jnp.einsum(

time: 98.4 us -> 90.4 us (0.919)
  between operations: 13.5 us -> 0.11 us
  other arithmetic: 9.47 us -> 14.1 us
  waiting for transfers between devices: 49.1 us -> 45 us
  starting transfers between devices: 9.9 us -> 14 us
    all_gather x1 -> x0, waiting for transfers between devices: 48.4 us -> none  [body(): panel = lax.all_gather(amplitudes, 'blk', axis=0, tiled=True)]
    ppermute x0 -> x2, waiting for transfers between devices: none -> 45 us  [doubled(): theirs = lax.ppermute(blocks, axis, [(i, i ^ bit) for i in range(devices)])]
    ppermute x0 -> x2, starting transfers between devices: none -> 5.61 us  [doubled(): theirs = lax.ppermute(blocks, axis, [(i, i ^ bit) for i in range(devices)])]
    another operation x0 -> x3, other arithmetic: none -> 2.88 us  [doubled(): both = jnp.stack([blocks, theirs])]
    select_n x0 -> x1, other arithmetic: none -> 1.87 us  [doubled(): blocks = jnp.where(upper == 0, both, both[::-1]).reshape(-1, *shard.shape)]
    all_to_all x1, starting transfers between devices: 5.17 us -> 3.72 us  [body(): lax.all_to_all(sent_coef, 'virt', split_axis=0, concat_axis=0, tiled=True)]
  transfers between devices with their start and end apart: 3 -> 4, of which waited for: 1 -> 1; matrix products, arithmetic and copies ran while one was open for 8% -> 20% of each run, Pallas kernels for 0% -> 0%
where the time goes in v1:
time: 90.4 us; the launch traced here: 90 us
  waiting for transfers between devices  45 us (50%)
  other arithmetic  14.1 us (16%)
  starting transfers between devices  14 us (15%)
  matrix products  9.29 us (10%)
  local copies, waits for them, and re-layouts  7.51 us (8%)
    ppermute x2, waiting for transfers between devices, doubled(): theirs = lax.ppermute(blocks, axis, [(i, i ^ bit) for i in range(devices)])  45 us
    ppermute x2, starting transfers between devices, doubled(): theirs = lax.ppermute(blocks, axis, [(i, i ^ bit) for i in range(devices)])  5.61 us
    dot_general x1, matrix products, body(): jnp.einsum('srp,stp->rtp', columns, product, precision=lax.Precision.HIGH...  4.99 us
    all_to_all x1, starting transfers between devices, body(): lax.all_to_all(sent_tiles, 'virt', split_axis=0, concat_axis=0, tiled=True)  4.67 us
    select_n x1, other arithmetic, body(): jnp.where(filled[:, None, None], integrals[source_tile], jnp.zeros((), jn...  4.49 us
    dot_general x1, matrix products, body(): jnp.einsum('stw,pw->stp', got_tiles, panel, preferred_element_type=jnp.fl...  4.15 us
    all_to_all x1, starting transfers between devices, body(): lax.all_to_all(sent_coef, 'virt', split_axis=0, concat_axis=0, tiled=True)  3.72 us
    another operation x3, other arithmetic, doubled(): both = jnp.stack([blocks, theirs])  2.88 us
  transfers between devices with their start and end apart: 4, of which 1 were waited for; matrix products, arithmetic and copies ran while one was open for 20% of the time, Pallas kernels for 0%

profile of v1, /device:TPU:0, one launch (start us, length us, event | category | flops | bytes accessed | tf_op | source)
XLA Modules:
  0.0 90.0 jit_solution(11145431066976472556)
XLA Ops:
  0.0 3.0 %collective-permute-start = (bf16[1,64,4096]{2,1,0:T(8,128)(2,1)}, bf16[1,64,4096]{2,1,0:T(8,128)(2,1)S(1)}, u32[]{:S(2)}, u32[]{:S(2)}) collective-permute-start(bf16[1,64,4096]{2,1,0:T(8,128)(2,1)} %bitcast.31), channel_id=1, source_target_pairs={{0,8},{8,0},{16,24},{24,16},{1,9},{9,1},{17,25},{25,17},{2,10},{10... | collective-permute-start | bytes 1572872 | tf_op jit(solution)/shard_map/ppermute | solution.py:18
  3.0 0.9 %convert_reduce_fusion = s32[16]{0:T(128)S(1)} fusion(s32[16]{0:T(128)} %param.11), kind=kLoop, calls=%fused_computation.20 | loop fusion | flops 1264 | bytes 128 | tf_op jit(solution)/shard_map/reduce_sum | solution.py:47
  3.9 0.7 multiply_add_fusion
  4.8 0.7 convert_element_type.25
  5.5 0.7 fusion.10
  6.3 0.6 gather_fusion.1
  6.9 0.7 select_convert_fusion
  7.6 3.7 %all-to-all-start.1 = ((bf16[8,4,16]{2,1,0:T(4,128)(2,1)}), bf16[8,4,16]{2,1,0:T(4,128)(2,1)S(1)}, u32[]{:S(2)}, u32[]{:S(2)}) async-start(bf16[8,4,16]{2,1,0:T(4,128)(2,1)} %select_convert_fusion), calls=%async_computation.1 | async-start | bytes 16384 | tf_op jit(solution)/shard_map/all_to_all | solution.py:65
  11.3 2.8 %gather_fusion = bf16[32,16,4096]{2,1,0:T(8,128)(2,1)} fusion(bf16[16,16,4096]{2,1,0:T(8,128)(2,1)S(1)} %copy-done, s32[1024]{0:T(1024)S(1)} %pad_clamp_fusion), kind=kCustom, calls=%fused_computation | custom fusion | bytes 8388736 | tf_op jit(solution)/shard_map/gather | solution.py:57
  14.1 4.5 %broadcast_select_fusion = bf16[32,16,4096]{2,1,0:T(8,128)(2,1)} fusion(bf16[32,16,4096]{2,1,0:T(8,128)(2,1)} %gather_fusion, pred[32]{0:T(512)(128)(4,1)S(1)} %fusion.5), kind=kLoop, calls=%fused_computation.2 | loop fusion | flops 2097152 | bytes 8388640 | tf_op jit(solution)/shard_map/jit(_where)/select_n | solution.py:56
  18.6 4.7 %all-to-all-start = ((bf16[32,16,4096]{2,1,0:T(8,128)(2,1)}), bf16[32,16,4096]{2,1,0:T(8,128)(2,1)}, u32[]{:S(2)}, u32[]{:S(2)}) async-start(bf16[32,16,4096]{2,1,0:T(8,128)(2,1)} %broadcast_select_fusion), calls=%async_computation | async-start | bytes 8388608 | tf_op jit(solution)/shard_map/all_to_all | solution.py:64
  23.5 1.4 %fusion.1 = (bf16[1,2,64,4096]{3,2,1,0:T(8,128)(2,1)S(1)}, bf16[2,64,4096]{2,1,0:T(8,128)(2,1)}) fusion(bf16[2,1,64,4096]{3,2,1,0:T(8,128)(2,1)S(1)} %pad_maximum_fusion.1, pred[]{:T(512)S(6)} %eq.95), kind=kLoop, calls=%fused_computation.13 | loop fusion | flops 524288 | bytes 3145729 | tf_op jit(solution)/shard_map/stack;reshape | solution.py:19
  24.8 2.6 %collective-permute-start.1 = (bf16[2,64,4096]{2,1,0:T(8,128)(2,1)}, bf16[2,64,4096]{2,1,0:T(8,128)(2,1)}, u32[]{:S(2)}, u32[]{:S(2)}) collective-permute-start(bf16[2,64,4096]{2,1,0:T(8,128)(2,1)} %get-tuple-element.8), channel_id=1, source_target_pairs={{0,16},{8,24},{16,0},{24,8},{1,17},{9,25},{17,1},{25,9},{2,18},{10... | collective-permute-start | bytes 3145736 | tf_op jit(solution)/shard_map/ppermute | solution.py:18
  27.4 0.4 select_reduce_fusion.1
  27.9 0.1 fusion.3
  28.0 1.0 %copy.23 = f32[32,4,256]{0,1,2:T(4,128)} copy(f32[32,4,256]{2,0,1:T(8,128)S(1)} %fusion.3) | data formatting | bytes 262144 | tf_op jit(solution)/shard_map/srk,kp->srp/dot_general | solution.py:71
  29.1 45.0 %collective-permute-done.1 = bf16[2,64,4096]{2,1,0:T(8,128)(2,1)} collective-permute-done((bf16[2,64,4096]{2,1,0:T(8,128)(2,1)}, bf16[2,64,4096]{2,1,0:T(8,128)(2,1)}, u32[]{:S(2)}, u32[]{:S(2)}) %collective-permute-start.1) | collective-permute-done | bytes 1048608 | tf_op jit(solution)/shard_map/ppermute | solution.py:18
  74.1 1.4 %pad_maximum_fusion = bf16[2,2,64,4096]{3,2,1,0:T(8,128)(2,1)S(1)} fusion(bf16[1,2,64,4096]{3,2,1,0:T(8,128)(2,1)} %bitcast.7, bf16[1,2,64,4096]{3,2,1,0:T(8,128)(2,1)S(1)} %get-tuple-element.7), kind=kLoop, calls=%fused_computation.4 | loop fusion | flops 1048576 | bytes 4194304 | tf_op jit(solution)/shard_map/stack | solution.py:19
  75.5 1.9 %reverse_select_fusion = bf16[2,2,64,4096]{3,2,1,0:T(8,128)(2,1)} fusion(bf16[2,2,64,4096]{3,2,1,0:T(8,128)(2,1)S(1)} %pad_maximum_fusion, pred[]{:T(512)S(6)} %eq.94), kind=kLoop, calls=%fused_computation.3 | loop fusion | flops 1048576 | bytes 4194305 | tf_op jit(solution)/shard_map/jit(_where)/select_n | solution.py:21
  77.3 4.2 %fusion.12 = f32[32,16,256]{2,1,0:T(8,128)S(1)} fusion(bf16[32,16,4096]{2,1,0:T(8,128)(2,1)} %all-to-all-done, bf16[256,4096,1]{1,0,2:T(8,128)(2,1)} %bitcast.30), kind=kOutput, calls=%fused_computation.39 | convolution fusion | flops 1073741824 | bytes 6815744 | tf_op jit(solution)/shard_map/stw,pw->stp/dot_general | solution.py:79
  81.5 2.6 %copy.22 = f32[32,16,256]{0,1,2:T(8,128)} copy(f32[32,16,256]{2,1,0:T(8,128)S(1)} %fusion.12) | data formatting | bytes 1048576 | tf_op jit(solution)/shard_map/stw,pw->stp/dot_general | solution.py:79
  84.1 5.0 %convolution_bitcast_fusion = f32[4,16,256]{1,0,2:T(4,128)S(1)} fusion(f32[32,16,256]{0,1,2:T(8,128)} %copy.22, f32[32,4,256]{0,1,2:T(4,128)S(1)} %copy-done.1), kind=kOutput, calls=%fused_computation.6 | convolution fusion | flops 6291456 | bytes 720896 | tf_op jit(solution)/shard_map/srp,stp->rtp/dot_general | solution.py:80
  89.1 0.2 copy.24
  89.3 0.7 fusion.2
  (27 shorter events, 0.6 us)
Async XLA Ops:
  0.0 11.3 %copy-start = (bf16[16,16,4096]{2,1,0:T(8,128)(2,1)S(1)}, bf16[16,16,4096]{2,1,0:T(8,128)(2,1)}, u32[]{:S(2)}) copy-start(bf16[16,16,4096]{2,1,0:T(8,128)(2,1)} %param.9) | copy-start | bytes 6291460
  0.0 23.3 %collective-permute-start = (bf16[1,64,4096]{2,1,0:T(8,128)(2,1)}, bf16[1,64,4096]{2,1,0:T(8,128)(2,1)S(1)}, u32[]{:S(2)}, u32[]{:S(2)}) collective-permute-start(bf16[1,64,4096]{2,1,0:T(8,128)(2,1)} %bitcast.31), channel_id=1, source_target_pairs={{0,8},{8,0},{16,24},{24,16},{1,9},{9,1},{17,25},{25,17},{2,10},{10... | collective-permute-start | bytes 1572872 | tf_op jit(solution)/shard_map/ppermute | solution.py:18
  7.6 11.0 %all-to-all-start.1 = ((bf16[8,4,16]{2,1,0:T(4,128)(2,1)}), bf16[8,4,16]{2,1,0:T(4,128)(2,1)S(1)}, u32[]{:S(2)}, u32[]{:S(2)}) async-start(bf16[8,4,16]{2,1,0:T(4,128)(2,1)} %select_convert_fusion), calls=%async_computation.1 | async-start | bytes 16384 | tf_op jit(solution)/shard_map/all_to_all | solution.py:65
  18.6 4.7 %copy-start.2 = (bf16[64,4096]{1,0:T(8,128)(2,1)S(1)}, bf16[64,4096]{1,0:T(8,128)(2,1)}, u32[]{:S(2)}) copy-start(bf16[64,4096]{1,0:T(8,128)(2,1)} %param.10) | copy-start | bytes 1572868
  18.6 58.7 %all-to-all-start = ((bf16[32,16,4096]{2,1,0:T(8,128)(2,1)}), bf16[32,16,4096]{2,1,0:T(8,128)(2,1)}, u32[]{:S(2)}, u32[]{:S(2)}) async-start(bf16[32,16,4096]{2,1,0:T(8,128)(2,1)} %broadcast_select_fusion), calls=%async_computation | async-start | bytes 8388608 | tf_op jit(solution)/shard_map/all_to_all | solution.py:64
  23.4 4.0 %copy-start.3 = (f32[1200]{0:T(1024)S(1)}, f32[1200]{0:T(1024)}, u32[]{:S(2)}) copy-start(f32[1200]{0:T(1024)} %param.15) | copy-start | bytes 14404
  23.4 4.0 %copy-start.4 = (s32[256]{0:T(256)S(1)}, s32[256]{0:T(256)}, u32[]{:S(2)}) copy-start(s32[256]{0:T(256)} %param.16) | copy-start | bytes 3076
  23.4 4.0 %copy-start.5 = (s32[256]{0:T(256)S(1)}, s32[256]{0:T(256)}, u32[]{:S(2)}) copy-start(s32[256]{0:T(256)} %param.17) | copy-start | bytes 3076
  24.8 49.2 %collective-permute-start.1 = (bf16[2,64,4096]{2,1,0:T(8,128)(2,1)}, bf16[2,64,4096]{2,1,0:T(8,128)(2,1)}, u32[]{:S(2)}, u32[]{:S(2)}) collective-permute-start(bf16[2,64,4096]{2,1,0:T(8,128)(2,1)} %get-tuple-element.8), channel_id=1, source_target_pairs={{0,16},{8,24},{16,0},{24,8},{1,17},{9,25},{17,1},{25,9},{2,18},{10... | collective-permute-start | bytes 3145736 | tf_op jit(solution)/shard_map/ppermute | solution.py:18
  81.5 2.6 %copy-start.1 = (f32[32,4,256]{0,1,2:T(4,128)S(1)}, f32[32,4,256]{0,1,2:T(4,128)}, u32[]{:S(2)}) copy-start(f32[32,4,256]{0,1,2:T(4,128)} %copy.23) | copy-start | bytes 393220
  84.1 5.2 %copy-start.6 = (f32[64]{0:T(128)S(1)}, f32[64]{0:T(128)}, u32[]{:S(2)}) copy-start(f32[64]{0:T(128)} %param.14) | copy-start | bytes 772
